TPU v7x, 32 devices: a whole 2x2x4 slice. The times are simulated.
32 devices in a mesh: freq: 16 (over z, y, core), chan: 2 (over x).
Axes of the slice: x: 2, y: 2, z: 4, core: 2. Of those that a mesh axis runs over, the one named last changes fastest.
Arguments:
- traces: bfloat16 [256, 2048, 256], P('freq', 'chan'), may hold values from -6 to 6
- channel_mask: int32 [2048], P('chan'), may hold values 0 or 1
- bin_index: int32 [16], replicated, may hold values from 1 to 127
Outputs:
- cross: bfloat16 [16, 2, 2048, 2048], P('freq', None, 'chan')
All inputs are finite; a program needn't handle non-finite values. No bound on the sum of `channel_mask` on one device may be relied on, other than what follows from the above.
Results may differ from a plain program's by a relative error of at most 0.0064.
Values may be sent and summed in bfloat16 or wider, within the bound.
No kernel may reach another device: no remote copies, remote signals or barrier semaphores. Data moves between devices by JAX's collectives and lax.ppermute only.
A program may use at most 64 MiB of HBM per device.

v0:
```python
import math

import jax
import jax.numpy as jnp
from jax import lax
from jax.sharding import PartitionSpec as P


def passed_along(value, axis, steps):
    count = lax.axis_size(axis)
    pairs = [(source, (source + steps) % count) for source in range(count)]
    return lax.ppermute(value, axis, pairs)


def shards(traces, channel_mask, bin_index):
    segment_local_rows, width, length = traces.shape
    nbins = bin_index.shape[0]
    samples = jnp.arange(length, dtype=jnp.int32)
    phase_index = bin_index[None, :] * samples[:, None] % length
    angles = 2.0 * math.pi / length * phase_index.astype(jnp.float32)
    wave_table = (
        jnp.stack([jnp.cos(angles), -jnp.sin(angles)], axis=2)
        .reshape(length, 2 * nbins)
        .astype(jnp.bfloat16)
    )
    taper_curve = 0.5 - 0.5 * jnp.cos(2.0 * math.pi / length * (samples.astype(jnp.float32) + 0.5))
    channel_gain = channel_mask.astype(jnp.float32)
    squares = jnp.einsum("sct,sct->sc", traces, traces, preferred_element_type=jnp.float32)
    spread = jnp.sqrt(squares / length + 1e-06)
    tapered = (
        traces.astype(jnp.float32)
        / spread[:, :, None]
        * taper_curve[None, None, :]
        * channel_gain[None, :, None]
    ).astype(jnp.bfloat16)
    segment_spectra = jnp.dot(
        tapered.reshape(segment_local_rows * width, length),
        wave_table,
        preferred_element_type=jnp.float32,
    )
    segment_spectra = segment_spectra.reshape(segment_local_rows, width, nbins, 2).transpose(
        2, 0, 3, 1
    )
    segment_spectra = lax.all_to_all(
        segment_spectra, "freq", split_axis=0, concat_axis=1, tiled=True
    )
    bins_local = segment_spectra.shape[0]
    segments = segment_spectra.shape[1]
    band_power = jnp.sum(segment_spectra * segment_spectra, axis=(1, 2)) / segments + 1e-06
    whitened = (segment_spectra / jnp.sqrt(band_power)[:, None, None, :]).astype(jnp.bfloat16)
    real_rows = whitened.reshape(bins_local, 2 * segments, width)
    turned = jnp.stack([whitened[:, :, 1], -whitened[:, :, 0]], axis=2).reshape(
        bins_local, 2 * segments, width
    )
    stacked_spectra = jnp.concatenate([real_rows, turned], axis=2)
    inverse = 1.0 / segments

    def block_cross_product(spectrum_fragment):
        cross_product_term = jnp.einsum(
            "mqr,mqe->mre", stacked_spectra, spectrum_fragment, preferred_element_type=jnp.float32
        )
        return (
            (cross_product_term * inverse)
            .reshape(bins_local, 2, width, spectrum_fragment.shape[2])
            .astype(jnp.bfloat16)
        )

    def place(result, spectrum_fragment, column):
        return lax.dynamic_update_slice(
            result, block_cross_product(spectrum_fragment), (0, 0, 0, column)
        )

    group = lax.axis_size("chan")
    own_index = lax.axis_index("chan")
    result = jnp.zeros((bins_local, 2, width, group * width), jnp.bfloat16)
    result = place(result, real_rows, own_index * width)
    moving = real_rows
    for step in range(1, group):
        moving = passed_along(moving, "chan", 1)
        result = place(result, moving, (own_index - step) % group * width)
    return result


def solution(mesh):
    in_specs = (P("freq", "chan", None), P("chan"), P())
    out_specs = P("freq", None, "chan", None)
    return jax.shard_map(shards, mesh=mesh, in_specs=in_specs, out_specs=out_specs, check_vma=False)
```

profile of v0, /device:TPU:14, one launch (start us, length us, event | category | flops | bytes accessed | tf_op | source)
XLA Modules:
  0.0 106.8 jit_solution(10640829522992178758)
XLA Ops:
  0.0 0.8 cosine_convert_fusion
  0.9 0.0 copy-start.3
  0.9 0.0 copy-start
  1.0 5.8 %fusion.3 = f32[16,1024]{1,0:T(8,128)S(1)} fusion(bf16[16,1024,256]{2,1,0:T(8,128)(2,1)} %param.3), kind=kLoop, calls=%fused_computation.5 | loop fusion | flops 12566528 | bytes 8454144 | tf_op jit(solution)/shard_map/sct,sct->sc/dot_general | solution.py:28
  6.8 0.0 copy-done.3
  6.8 0.0 copy-done
  6.8 3.3 %fusion.8 = f32[16,16,2,1024]{3,0,2,1:T(8,128)S(1)} fusion(bf16[16,1024,256]{2,1,0:T(8,128)(2,1)S(1)} %copy-done, f32[1024]{0:T(1024)S(1)} %convert_element_type.90, f32[256]{0:T(256)S(1)} %multiply_subtract_fusion, f32[16,1024]{1,0:T(8,128)S(1)} %add_sqrt_fusion, bf16[16,2,256]{2,1,0:T(2,128)(2,1)S(1)} %dot_general.18), kind=kOutput, calls=%fused_computation.16 | convolution fusion | flops 289406976 | bytes 10572800 | tf_op jit(solution)/shard_map/dot_general | solution.py:36
  10.1 2.9 %copy.15 = f32[16,16,2,1024]{3,2,1,0:T(2,128)} copy(f32[16,16,2,1024]{3,0,2,1:T(8,128)S(1)} %fusion.8) | data formatting | bytes 4194304 | tf_op jit(solution)/shard_map/transpose | solution.py:41
  13.0 6.2 %all-to-all-start = ((f32[16,16,2,1024]{3,2,1,0:T(2,128)}), f32[16,16,2,1024]{3,2,1,0:T(2,128)S(1)}, u32[]{:S(2)}, u32[]{:S(2)}) async-start(f32[16,16,2,1024]{3,2,1,0:T(2,128)} %copy.15), calls=%async_computation | async-start | bytes 4194304 | tf_op jit(solution)/shard_map/all_to_all | solution.py:44
  19.3 47.1 %all-to-all-done = f32[16,16,2,1024]{3,2,1,0:T(2,128)S(1)} async-done(((f32[16,16,2,1024]{3,2,1,0:T(2,128)}), f32[16,16,2,1024]{3,2,1,0:T(2,128)S(1)}, u32[]{:S(2)}, u32[]{:S(2)}) %all-to-all-start) | async-done | bytes 2097184 | tf_op jit(solution)/shard_map/all_to_all | solution.py:44
  66.4 0.9 multiply_reduce_fusion
  67.3 0.7 copy.16
  68.0 1.2 %fusion.7 = bf16[1,256,2,1024]{3,1,2,0:T(8,128)(2,1)} fusion(f32[16,16,2,1024]{3,1,0,2:T(8,128)S(1)} %copy.16, f32[1024]{0:T(1024)S(1)} %add_sqrt_fusion.1), kind=kLoop, calls=%fused_computation.12 | loop fusion | flops 1048576 | bytes 3149824 | tf_op jit(solution)/shard_map/convert_element_type | solution.py:50
  69.2 2.4 %all_to_all.12 = f32[1,512,1024]{2,1,0:T(8,128)} reshape(f32[16,16,2,1024]{3,2,1,0:T(2,128)S(1)} %all-to-all-done) | data formatting | bytes 4194304 | tf_op jit(solution)/shard_map/all_to_all | solution.py:44
  71.7 0.0 copy-start.2
  71.7 2.9 %divide_convert_fusion = bf16[1,512,1024]{2,1,0:T(8,128)(2,1)} fusion(f32[1,512,1024]{2,1,0:T(8,128)} %all_to_all.12, f32[1024]{0:T(1024)S(1)} %add_sqrt_fusion.1), kind=kLoop, calls=%fused_computation.13 | loop fusion | flops 1048576 | bytes 3149824 | tf_op jit(solution)/shard_map/convert_element_type | solution.py:50
  74.6 0.5 collective-permute-start
  75.1 0.9 divide_convert_fusion.1
  76.0 0.0 copy-done.2
  76.0 0.1 fusion.22
  76.1 0.1 pad_maximum_fusion
  76.2 1.1 %copy.17 = bf16[1,256,2,1024]{3,2,1,0:T(2,128)(2,1)S(1)} copy(bf16[1,256,2,1024]{3,1,2,0:T(8,128)(2,1)S(1)} %pad_maximum_fusion) | data formatting | bytes 2097152 | tf_op jit(solution)/shard_map/stack | solution.py:52
  77.3 0.4 reshape.233
  77.7 0.4 convert_element_type.97
  78.2 3.6 %multiply_convert_fusion.1 = bf16[2048,1024]{1,0:T(8,128)(2,1)S(1)} fusion(bf16[512,1024]{1,0:T(8,128)(2,1)S(1)} %convert_element_type.97, bf16[1,512,1024]{2,1,0:T(8,128)(2,1)S(1)} %reshape.233, bf16[1,512,1024]{2,1,0:T(8,128)(2,1)} %divide_convert_fusion), kind=kOutput, calls=%fused_computation.8 | convolution fusion | flops 2155872256 | bytes 7340032 | tf_op jit(solution)/shard_map/mqr,mqe->mre/dot_general | solution.py:59
  81.8 1.1 broadcast_in_dim.2
  82.9 0.6 constant_dynamic-update-slice_fusion.1
  83.5 0.0 copy-start.1
  83.5 16.9 %collective-permute-done = bf16[1,512,1024]{2,1,0:T(8,128)(2,1)} collective-permute-done((bf16[1,512,1024]{2,1,0:T(8,128)(2,1)}, bf16[1,512,1024]{2,1,0:T(8,128)(2,1)}, u32[]{:S(2)}, u32[]{:S(2)}) %collective-permute-start) | collective-permute-done | bytes 1048608 | tf_op jit(solution)/shard_map/ppermute | solution.py:12
  100.4 3.9 %multiply_convert_fusion = bf16[2048,1024]{1,0:T(8,128)(2,1)S(1)} fusion(bf16[1,512,1024]{2,1,0:T(8,128)(2,1)S(1)} %reshape.233, bf16[1,512,1024]{2,1,0:T(8,128)(2,1)} %divide_convert_fusion, bf16[1,512,1024]{2,1,0:T(8,128)(2,1)} %collective-permute-done), kind=kOutput, calls=%fused_computation.7 | convolution fusion | flops 2155872256 | bytes 7340032 | tf_op jit(solution)/shard_map/mqr,mqe->mre/dot_general | solution.py:59
  104.3 0.0 copy-done.1
  104.3 2.5 %constant_dynamic-update-slice_fusion = bf16[1,2,1024,2048]{3,2,1,0:T(8,128)(2,1)} fusion(bf16[1,2,1024,2048]{3,2,1,0:T(8,128)(2,1)} %copy-done.1, bf16[1,2,1024,1024]{3,2,1,0:T(8,128)(2,1)S(1)} %bitcast.29, s32[]{:T(128)S(6)} %select_n.33), kind=kLoop, calls=%fused_computation.37 | loop fusion | bytes 8388612 | tf_op jit(solution)/shard_map/dynamic_update_slice | solution.py:69
  (8 shorter events, 0.1 us)
Async XLA Ops:
  0.9 5.8 %copy-start.3 = (s32[1024]{0:T(1024)S(1)}, s32[1024]{0:T(1024)}, u32[]{:S(2)}) copy-start(s32[1024]{0:T(1024)} %param.4) | copy-start | bytes 12292
  0.9 5.8 %copy-start = (bf16[16,1024,256]{2,1,0:T(8,128)(2,1)S(1)}, bf16[16,1024,256]{2,1,0:T(8,128)(2,1)}, u32[]{:S(2)}) copy-start(bf16[16,1024,256]{2,1,0:T(8,128)(2,1)} %param.3) | copy-start | bytes 25165828
  13.0 53.4 %all-to-all-start = ((f32[16,16,2,1024]{3,2,1,0:T(2,128)}), f32[16,16,2,1024]{3,2,1,0:T(2,128)S(1)}, u32[]{:S(2)}, u32[]{:S(2)}) async-start(f32[16,16,2,1024]{3,2,1,0:T(2,128)} %copy.15), calls=%async_computation | async-start | bytes 4194304 | tf_op jit(solution)/shard_map/all_to_all | solution.py:44
  71.7 4.4 %copy-start.2 = (bf16[1,256,2,1024]{3,1,2,0:T(8,128)(2,1)S(1)}, bf16[1,256,2,1024]{3,1,2,0:T(8,128)(2,1)}, u32[]{:S(2)}) copy-start(bf16[1,256,2,1024]{3,1,2,0:T(8,128)(2,1)} %fusion.7) | copy-start | bytes 3145732
  74.6 25.8 %collective-permute-start = (bf16[1,512,1024]{2,1,0:T(8,128)(2,1)}, bf16[1,512,1024]{2,1,0:T(8,128)(2,1)}, u32[]{:S(2)}, u32[]{:S(2)}) collective-permute-start(bf16[1,512,1024]{2,1,0:T(8,128)(2,1)} %divide_convert_fusion), channel_id=1, source_target_pairs={{0,1},{1,0},{2,3},{3,2},{4,5},{5,4},{6,7},{7,6},{8,9},{9,8},{10,11... | collective-permute-start | bytes 3145736 | tf_op jit(solution)/shard_map/ppermute | solution.py:12
  83.5 20.8 %copy-start.1 = (bf16[1,2,1024,2048]{3,2,1,0:T(8,128)(2,1)}, bf16[1,2,1024,2048]{3,2,1,0:T(8,128)(2,1)S(1)}, u32[]{:S(2)}) copy-start(bf16[1,2,1024,2048]{3,2,1,0:T(8,128)(2,1)S(1)} %constant_dynamic-update-slice_fusion.1) | copy-start | bytes 25165828
where the time goes:
time: 107 us
  waiting for transfers between devices  64 us (60%)
  other arithmetic  12.8 us (12%)
  local copies, waits for them, and re-layouts  12.2 us (11%)
  matrix products  10.8 us (10%)
  starting transfers between devices  6.78 us (6%)
    all_to_all x1, waiting for transfers between devices, shards(): lax.all_to_all(segment_spectra, 'freq', split_axis=0, concat_axis=1, tile...  47.1 us
    ppermute x1, waiting for transfers between devices, passed_along(): return lax.ppermute(value, axis, pairs)  16.9 us
    dot_general x2, matrix products, block_cross_product(): jnp.einsum('mqr,mqe->mre', stacked_spectra, spectrum_fragment, preferred_...  7.53 us
    all_to_all x1, starting transfers between devices, shards(): lax.all_to_all(segment_spectra, 'freq', split_axis=0, concat_axis=1, tile...  6.24 us
    dot_general x1, other arithmetic, shards(): jnp.einsum('sct,sct->sc', traces, traces, preferred_element_type=jnp.floa...  5.77 us
    convert_element_type x3, other arithmetic, shards(): (segment_spectra / jnp.sqrt(band_power)[:, None, None, :]).astype(jnp.bfl...  5.04 us
    dot_general x1, matrix products, shards(): jnp.dot(tapered.reshape(segment_local_rows * width, length), wave_table,...  3.3 us
    all_to_all x2, local copies, waits for them, and re-layouts, shards(): lax.all_to_all(segment_spectra, 'freq', split_axis=0, concat_axis=1, tile...  3.09 us
  transfers between devices with their start and end apart: 2, of which 2 were waited for; matrix products, arithmetic and copies ran while one was open for 8% of the time, Pallas kernels for 0%

commit v1 on v0

v1 whole, which is shorter than its diff:
```python
import functools
import math

import jax
import jax.numpy as jnp
from jax import lax
from jax.experimental import pallas as pl
from jax.experimental.pallas import tpu as pltpu
from jax.sharding import PartitionSpec as P

LANES = 128
SHARES = (5, 3)


def passed_along(value, axis, steps):
    count = lax.axis_size(axis)
    pairs = [(source, (source + steps) % count) for source in range(count)]
    return lax.ppermute(value, axis, pairs)


def divisor(value, limit):
    return max(d for d in range(1, min(value, limit) + 1) if value % d == 0)


def pieces(width):
    units = width // LANES
    if units < 2:
        return [(0, width)]
    first = min(max(1, round(units * SHARES[0] / sum(SHARES))), units - 1)
    return [(0, first * LANES), (first * LANES, width - first * LANES)]


def spectra_kernel(batch, segments, table_ref, taper_ref, gain_ref, traces_ref, out_ref, held):
    step = pl.program_id(0)
    rows, length = table_ref.shape
    taper = taper_ref[...]
    for place in range(batch):
        record = traces_ref[place].astype(jnp.float32)
        squares = jnp.sum(record * record, axis=1, keepdims=True)
        inverse = lax.rsqrt(squares / length + 1e-06)
        tapered = (record * inverse * taper).astype(jnp.bfloat16)
        spectra = lax.dot_general(
            table_ref[...], tapered, (((1,), (1,)), ((), ())), preferred_element_type=jnp.float32
        )
        spectra = spectra * gain_ref[...]
        for tile in range(held.shape[0]):
            kept = spectra[:, tile * LANES : (tile + 1) * LANES]
            held[tile, pl.ds(step * batch + place, rows, stride=segments), :] = kept

    @pl.when(step == pl.num_programs(0) - 1)
    def _():
        for tile in range(held.shape[0]):
            out_ref[:, tile * LANES : (tile + 1) * LANES] = held[tile].astype(jnp.bfloat16)


def spectra_of(traces, gain, table, taper, start, size):
    segments, width, length = traces.shape
    rows = table.shape[0]
    batch = divisor(segments, 4)
    return pl.pallas_call(
        functools.partial(spectra_kernel, batch, segments),
        grid=(segments // batch,),
        in_specs=[
            pl.BlockSpec((rows, length), lambda i: (0, 0)),
            pl.BlockSpec((1, length), lambda i: (0, 0)),
            pl.BlockSpec((pl.Element(1), pl.Element(size)), lambda i: (0, start)),
            pl.BlockSpec(
                (pl.Element(batch), pl.Element(size), pl.Element(length)),
                lambda i: (i * batch, start, 0),
            ),
        ],
        out_specs=pl.BlockSpec((rows * segments, size), lambda i: (0, 0)),
        out_shape=jax.ShapeDtypeStruct((rows * segments, size), jnp.bfloat16),
        scratch_shapes=[pltpu.VMEM((size // LANES, rows * segments, LANES), jnp.float32)],
        cost_estimate=pl.CostEstimate(
            flops=2 * rows * segments * size * length,
            bytes_accessed=2 * segments * size * length,
            transcendentals=0,
        ),
    )(table, taper, gain, traces)


def column_scale(values, segments):
    wide = values.astype(jnp.float32)
    return lax.rsqrt(jnp.sum(wide * wide, axis=0, keepdims=True) / segments + 1e-06)


def row_scale(values, segments):
    wide = values.astype(jnp.float32)
    return lax.rsqrt(jnp.sum(wide * wide, axis=1, keepdims=True) / segments + 1e-06)


def own_kernel(local, segments, count, place_ref, *refs):
    own_refs, (out_ref, left_ref, whole, across) = refs[:count], refs[count:]
    step = pl.program_id(0)

    @pl.when(step == 0)
    def _():
        start = 0
        for ref in own_refs:
            size = ref.shape[1]
            whole[:, start : start + size] = ref[...]
            start += size
        across[...] = column_scale(whole[...], segments)

    rows = out_ref.shape[2]
    block = whole[:, pl.ds(pl.multiple_of(step * rows, rows), rows)]
    parts = block.reshape(block.shape[0] // (2 * local), 2, local, rows)
    turned = jnp.concatenate([parts[:, 1:], -parts[:, :1]], axis=1).reshape(block.shape)
    plain_left = block.T
    turned_left = turned.T
    left_ref[0] = plain_left
    left_ref[1] = turned_left
    scale = row_scale(plain_left, segments) * (1.0 / segments)
    for part, left in enumerate((plain_left, turned_left)):
        product = jnp.dot(left, whole[...], preferred_element_type=jnp.float32)
        out_ref[0, part] = (product * scale * across[...]).astype(jnp.bfloat16)


def own_blocks(own, local, place, bins_local, group):
    depth = own[0].shape[0]
    width = sum(piece.shape[1] for piece in own)
    segments = depth // 2
    rows = divisor(width, 256)
    return pl.pallas_call(
        functools.partial(own_kernel, local, segments, len(own)),
        grid_spec=pltpu.PrefetchScalarGridSpec(
            num_scalar_prefetch=1,
            grid=(width // rows,),
            in_specs=[pl.BlockSpec(piece.shape, lambda i, at: (0, 0)) for piece in own],
            out_specs=[
                pl.BlockSpec((1, 2, rows, width), lambda i, at: (0, 0, i, at[0])),
                pl.BlockSpec((2, rows, depth), lambda i, at: (0, i, 0)),
            ],
            scratch_shapes=[pltpu.VMEM((depth, width), jnp.bfloat16), pltpu.VMEM((1, width), jnp.float32)],
        ),
        out_shape=[
            jax.ShapeDtypeStruct((bins_local, 2, width, group * width), jnp.bfloat16),
            jax.ShapeDtypeStruct((2, width, depth), jnp.bfloat16),
        ],
        cost_estimate=pl.CostEstimate(
            flops=4 * width * width * depth, bytes_accessed=4 * width * width, transcendentals=0
        ),
    )(place, *own)


def peer_kernel(segments, place_ref, left_ref, peer_ref, result_ref, out_ref, across):
    @pl.when(pl.program_id(0) == 0)
    def _():
        across[...] = column_scale(peer_ref[...], segments)

    scale = row_scale(left_ref[0], segments) * (1.0 / segments)
    for part in range(2):
        product = jnp.dot(left_ref[part], peer_ref[...], preferred_element_type=jnp.float32)
        out_ref[0, part] = (product * scale * across[...]).astype(jnp.bfloat16)


def peer_blocks(result, left, peer, place, unit):
    depth, size = peer.shape
    width = left.shape[1]
    rows = divisor(width, 256)
    return pl.pallas_call(
        functools.partial(peer_kernel, depth // 2),
        grid_spec=pltpu.PrefetchScalarGridSpec(
            num_scalar_prefetch=1,
            grid=(width // rows,),
            in_specs=[
                pl.BlockSpec((2, rows, depth), lambda i, at: (0, i, 0)),
                pl.BlockSpec((depth, size), lambda i, at: (0, 0)),
                pl.BlockSpec(memory_space=pl.ANY),
            ],
            out_specs=pl.BlockSpec(
                (pl.Element(1), pl.Element(2), pl.Element(rows), pl.Element(size)),
                lambda i, at: (0, 0, i * rows, pl.multiple_of(at[0] * unit, unit)),
            ),
            scratch_shapes=[pltpu.VMEM((1, size), jnp.float32)],
        ),
        out_shape=jax.ShapeDtypeStruct(result.shape, result.dtype),
        input_output_aliases={3: 0},
        cost_estimate=pl.CostEstimate(
            flops=4 * width * size * depth, bytes_accessed=4 * width * size, transcendentals=0
        ),
    )(place, left, peer, result)


def shards(traces, channel_mask, bin_index):
    local, width, length = traces.shape
    nbins = bin_index.shape[0]
    samples = jnp.arange(length, dtype=jnp.int32)
    phase_index = bin_index[:, None, None] * samples[None, None, :] % length
    angles = 2.0 * math.pi / length * phase_index.astype(jnp.float32)
    real_part = jnp.arange(2, dtype=jnp.int32)[None, :, None] == 0
    table = jnp.where(real_part, jnp.cos(angles), -jnp.sin(angles))
    table = table.reshape(2 * nbins, length).astype(jnp.bfloat16)
    taper = 0.5 - 0.5 * jnp.cos(2.0 * math.pi / length * (samples.astype(jnp.float32) + 0.5))
    gain = channel_mask.astype(jnp.float32)[None, :]

    freq = lax.axis_size("freq")
    group = lax.axis_size("chan")
    own_index = lax.axis_index("chan")
    assert nbins == freq
    cuts = pieces(width)
    own = []
    for start, size in cuts:
        spectra = spectra_of(traces, gain, table, taper[None, :], start, size)
        blocks = spectra.reshape(nbins, 2 * local, size)
        arrived = lax.all_to_all(blocks, "freq", split_axis=0, concat_axis=0, tiled=True)
        own.append(arrived.reshape(freq * 2 * local, size))
    result, left = own_blocks(own, local, own_index[None].astype(jnp.int32), 1, group)
    moving = own
    for step in range(1, group):
        moving = [passed_along(piece, "chan", 1) for piece in moving]
        owner = (own_index - step) % group
        for (start, size), piece in zip(cuts, moving):
            unit = math.gcd(start, width)
            place = (owner * width + start) // unit
            result = peer_blocks(result, left, piece, place[None].astype(jnp.int32), unit)
    return result


def solution(mesh):
    in_specs = (P("freq", "chan", None), P("chan"), P())
    out_specs = P("freq", None, "chan", None)
    return jax.shard_map(shards, mesh=mesh, in_specs=in_specs, out_specs=out_specs, check_vma=False)
```

time: 107 us -> 70.3 us (0.66)
  the two profiles are of different devices: /device:TPU:14 before, /device:TPU:0 now
where the time goes in v1:
time: 70.3 us; the launch traced here: 69.6 us
  Pallas kernels  26.8 us (38%)
  waiting for transfers between devices  22.5 us (32%)
  starting transfers between devices  15.1 us (21%)
  other arithmetic  3.39 us (5%)
  local copies, waits for them, and re-layouts  1.76 us (3%)
    all_to_all x2, waiting for transfers between devices, shards(): lax.all_to_all(blocks, 'freq', split_axis=0, concat_axis=0, tiled=True)  22.5 us
    all_to_all x2, starting transfers between devices, shards(): lax.all_to_all(blocks, 'freq', split_axis=0, concat_axis=0, tiled=True)  12.1 us
    pallas_call x2, Pallas kernels, spectra_of(): pl.pallas_call(functools.partial(spectra_kernel, batch, segments), grid=(...  10.7 us
    pallas_call x2, Pallas kernels, peer_blocks(): pl.pallas_call(functools.partial(peer_kernel, depth // 2), grid_spec=pltp...  10 us
    pallas_call x1, Pallas kernels, own_blocks(): pl.pallas_call(functools.partial(own_kernel, local, segments, len(own)),...  5.99 us
    ppermute x2, starting transfers between devices, passed_along(): return lax.ppermute(value, axis, pairs)  3.05 us
    unnamed x8, local copies, waits for them, and re-layouts  1.61 us
  transfers between devices with their start and end apart: 4, of which 2 were waited for; matrix products, arithmetic and copies ran while one was open for 0% of the time, Pallas kernels for 23%

profile of v1, /device:TPU:0, one launch (start us, length us, event | category | flops | bytes accessed | tf_op | source)
XLA Modules:
  0.0 69.6 jit_solution(14049634274012486882)
XLA Ops:
  0.0 0.6 multiply_subtract_fusion.taper_ref
  0.6 0.1 broadcast_in_dim.52
  0.7 1.3 %convert_element_type.32 = f32[1024]{0:T(1024)} convert(s32[1024]{0:T(1024)} %param.4) | non-fusion elementwise | flops 1024 | bytes 8192 | tf_op jit(solution)/shard_map/convert_element_type | solution.py:196
  2.0 0.8 %sine_negate_fusion = (bf16[16,256]{1,0:T(8,128)(2,1)S(1)}, bf16[16,256]{1,0:T(8,128)(2,1)S(1)}) fusion(s32[16]{0:T(128)} %param.5), kind=kLoop, calls=%fused_computation.7 | loop fusion | flops 69632 | bytes 16448 | tf_op jit(solution)/shard_map/neg | solution.py:193
  2.9 0.7 select_convert_fusion.table_ref
  3.6 6.1 %shard_map.37 = bf16[512,640]{1,0:T(8,128)(2,1)} custom-call(bf16[32,256]{1,0:T(8,128)(2,1)} %select_convert_fusion.table_ref, f32[1,256]{1,0:T(1,128)} %multiply_subtract_fusion.taper_ref, f32[1,1024]{1,0:T(1,128)} %bitcast.14, bf16[16,1024,256]{2,1,0:T(8,128)(2,1)} %traces_ref.3), custom_call_target="tpu_custom_call" | custom-call | flops 167772160 | bytes 5242880 | tf_op jit(solution)/shard_map/pallas_call | solution.py:60
  9.6 7.4 %all-to-all-start = ((bf16[16,32,640]{2,1,0:T(8,128)(2,1)}), bf16[16,32,640]{2,1,0:T(8,128)(2,1)S(1)}, u32[]{:S(2)}, u32[]{:S(2)}) async-start(bf16[16,32,640]{2,1,0:T(8,128)(2,1)} %bitcast.8), calls=%async_computation | async-start | bytes 1310720 | tf_op jit(solution)/shard_map/all_to_all | solution.py:207
  17.1 4.7 %shard_map.38 = bf16[512,384]{1,0:T(8,128)(2,1)} custom-call(bf16[32,256]{1,0:T(8,128)(2,1)} %select_convert_fusion.table_ref, f32[1,256]{1,0:T(1,128)} %multiply_subtract_fusion.taper_ref, f32[1,1024]{1,0:T(1,128)} %bitcast.15, bf16[16,1024,256]{2,1,0:T(8,128)(2,1)} %traces_ref.3), custom_call_target="tpu_custom_call" | custom-call | flops 100663296 | bytes 3145728 | tf_op jit(solution)/shard_map/pallas_call | solution.py:60
  21.7 11.9 %all-to-all-done = bf16[16,32,640]{2,1,0:T(8,128)(2,1)S(1)} async-done(((bf16[16,32,640]{2,1,0:T(8,128)(2,1)}), bf16[16,32,640]{2,1,0:T(8,128)(2,1)S(1)}, u32[]{:S(2)}, u32[]{:S(2)}) %all-to-all-start) | async-done | bytes 655392 | tf_op jit(solution)/shard_map/all_to_all | solution.py:207
  33.6 0.0 copy-start.1
  33.6 4.7 %all-to-all-start.1 = ((bf16[16,32,384]{2,1,0:T(8,128)(2,1)}), bf16[16,32,384]{2,1,0:T(8,128)(2,1)S(1)}, u32[]{:S(2)}, u32[]{:S(2)}) async-start(bf16[16,32,384]{2,1,0:T(8,128)(2,1)} %bitcast.9), calls=%async_computation.1 | async-start | bytes 786432 | tf_op jit(solution)/shard_map/all_to_all | solution.py:207
  38.3 1.6 %collective-permute-start.1 = (bf16[512,640]{1,0:T(8,128)(2,1)S(1)}, bf16[512,640]{1,0:T(8,128)(2,1)S(1)}, u32[]{:S(2)}, u32[]{:S(2)}) collective-permute-start(bf16[512,640]{1,0:T(8,128)(2,1)S(1)} %bitcast.10), channel_id=1, source_target_pairs={{0,1},{1,0},{2,3},{3,2},{4,5},{5,4},{6,7},{7,6},{8,9},{9,8},{10,11... | collective-permute-start | bytes 1966088 | tf_op jit(solution)/shard_map/ppermute | solution.py:18
  39.9 10.6 %all-to-all-done.1 = bf16[16,32,384]{2,1,0:T(8,128)(2,1)S(1)} async-done(((bf16[16,32,384]{2,1,0:T(8,128)(2,1)}), bf16[16,32,384]{2,1,0:T(8,128)(2,1)S(1)}, u32[]{:S(2)}, u32[]{:S(2)}) %all-to-all-start.1) | async-done | bytes 393248 | tf_op jit(solution)/shard_map/all_to_all | solution.py:207
  50.5 0.0 copy-start.2
  50.5 1.5 %collective-permute-start = (bf16[512,384]{1,0:T(8,128)(2,1)S(1)}, bf16[512,384]{1,0:T(8,128)(2,1)S(1)}, u32[]{:S(2)}, u32[]{:S(2)}) collective-permute-start(bf16[512,384]{1,0:T(8,128)(2,1)S(1)} %bitcast.12), channel_id=1, source_target_pairs={{0,1},{1,0},{2,3},{3,2},{4,5},{5,4},{6,7},{7,6},{8,9},{9,8},{10,11... | collective-permute-start | bytes 1179656 | tf_op jit(solution)/shard_map/ppermute | solution.py:18
  52.0 0.0 copy-done.1
  52.0 0.0 copy-done.2
  52.0 6.0 %shard_map.39 = (bf16[1,2,1024,2048]{3,2,1,0:T(8,128)(2,1)}, bf16[2,1024,512]{2,1,0:T(8,128)(2,1)}) custom-call(s32[1]{0:T(128)} %bitcast.1.place_ref, bf16[512,640]{1,0:T(8,128)(2,1)} %bitcast.11, bf16[512,384]{1,0:T(8,128)(2,1)} %bitcast.13), custom_call_target="tpu_custom_call" | custom-call | flops 2147483648 | bytes 4194304 | tf_op jit(solution)/shard_map/pallas_call | solution.py:125
  58.0 0.0 collective-permute-done.1.peer_ref
  58.0 0.0 copy-start
  58.0 0.8 %copy-done = bf16[512,640]{1,0:T(8,128)(2,1)} copy-done((bf16[512,640]{1,0:T(8,128)(2,1)}, bf16[512,640]{1,0:T(8,128)(2,1)S(1)}, u32[]{:S(2)}) %copy-start) | copy-done | bytes 655384
  58.8 5.3 %shard_map.40.result_ref = bf16[1,2,1024,2048]{3,2,1,0:T(8,128)(2,1)} custom-call(s32[1]{0:T(128)} %bitcast.7.place_ref, bf16[2,1024,512]{2,1,0:T(8,128)(2,1)} %get-tuple-element.7.left_ref, bf16[512,640]{1,0:T(8,128)(2,1)} %copy-done, bf16[1,2,1024,2048]{3,2,1,0:T(8,128)(2,1)} %get-tuple-element.8.result_ref), custom_call_target="tpu_custom_call", output_to_operand_aliasing={{}: (3, {})} | custom-call | flops 1342177280 | bytes 2621440 | tf_op jit(solution)/shard_map/pallas_call | solution.py:162
  64.1 0.0 collective-permute-done.peer_ref
  64.2 0.0 copy-start.3
  64.2 0.8 %copy-done.3 = bf16[512,384]{1,0:T(8,128)(2,1)} copy-done((bf16[512,384]{1,0:T(8,128)(2,1)}, bf16[512,384]{1,0:T(8,128)(2,1)S(1)}, u32[]{:S(2)}) %copy-start.3) | copy-done | bytes 393240
  64.9 4.7 %shard_map.41 = bf16[1,2,1024,2048]{3,2,1,0:T(8,128)(2,1)} custom-call(s32[1]{0:T(128)} %bitcast.place_ref, bf16[2,1024,512]{2,1,0:T(8,128)(2,1)} %get-tuple-element.7.left_ref, bf16[512,384]{1,0:T(8,128)(2,1)} %copy-done.3, bf16[1,2,1024,2048]{3,2,1,0:T(8,128)(2,1)} %shard_map.40.result_ref), custom_call_target="tpu_custom_call", output_to_operand_aliasing={{}: (3, {})} | custom-call | flops 805306368 | bytes 1572864 | tf_op jit(solution)/shard_map/pallas_call | solution.py:162
  (6 shorter events, 0.1 us)
Async XLA Ops:
  9.6 24.0 %all-to-all-start = ((bf16[16,32,640]{2,1,0:T(8,128)(2,1)}), bf16[16,32,640]{2,1,0:T(8,128)(2,1)S(1)}, u32[]{:S(2)}, u32[]{:S(2)}) async-start(bf16[16,32,640]{2,1,0:T(8,128)(2,1)} %bitcast.8), calls=%async_computation | async-start | bytes 1310720 | tf_op jit(solution)/shard_map/all_to_all | solution.py:207
  33.6 18.3 %copy-start.1 = (bf16[16,32,640]{2,1,0:T(8,128)(2,1)}, bf16[16,32,640]{2,1,0:T(8,128)(2,1)S(1)}, u32[]{:S(2)}) copy-start(bf16[16,32,640]{2,1,0:T(8,128)(2,1)S(1)} %all-to-all-done) | copy-start | bytes 1966084
  33.6 16.8 %all-to-all-start.1 = ((bf16[16,32,384]{2,1,0:T(8,128)(2,1)}), bf16[16,32,384]{2,1,0:T(8,128)(2,1)S(1)}, u32[]{:S(2)}, u32[]{:S(2)}) async-start(bf16[16,32,384]{2,1,0:T(8,128)(2,1)} %bitcast.9), calls=%async_computation.1 | async-start | bytes 786432 | tf_op jit(solution)/shard_map/all_to_all | solution.py:207
  38.3 19.7 %collective-permute-start.1 = (bf16[512,640]{1,0:T(8,128)(2,1)S(1)}, bf16[512,640]{1,0:T(8,128)(2,1)S(1)}, u32[]{:S(2)}, u32[]{:S(2)}) collective-permute-start(bf16[512,640]{1,0:T(8,128)(2,1)S(1)} %bitcast.10), channel_id=1, source_target_pairs={{0,1},{1,0},{2,3},{3,2},{4,5},{5,4},{6,7},{7,6},{8,9},{9,8},{10,11... | collective-permute-start | bytes 1966088 | tf_op jit(solution)/shard_map/ppermute | solution.py:18
  50.5 1.5 %copy-start.2 = (bf16[16,32,384]{2,1,0:T(8,128)(2,1)}, bf16[16,32,384]{2,1,0:T(8,128)(2,1)S(1)}, u32[]{:S(2)}) copy-start(bf16[16,32,384]{2,1,0:T(8,128)(2,1)S(1)} %all-to-all-done.1) | copy-start | bytes 1179652
  50.5 13.7 %collective-permute-start = (bf16[512,384]{1,0:T(8,128)(2,1)S(1)}, bf16[512,384]{1,0:T(8,128)(2,1)S(1)}, u32[]{:S(2)}, u32[]{:S(2)}) collective-permute-start(bf16[512,384]{1,0:T(8,128)(2,1)S(1)} %bitcast.12), channel_id=1, source_target_pairs={{0,1},{1,0},{2,3},{3,2},{4,5},{5,4},{6,7},{7,6},{8,9},{9,8},{10,11... | collective-permute-start | bytes 1179656 | tf_op jit(solution)/shard_map/ppermute | solution.py:18
  58.0 0.8 %copy-start = (bf16[512,640]{1,0:T(8,128)(2,1)}, bf16[512,640]{1,0:T(8,128)(2,1)S(1)}, u32[]{:S(2)}) copy-start(bf16[512,640]{1,0:T(8,128)(2,1)S(1)} %collective-permute-done.1.peer_ref) | copy-start | bytes 1966084
  64.2 0.8 %copy-start.3 = (bf16[512,384]{1,0:T(8,128)(2,1)}, bf16[512,384]{1,0:T(8,128)(2,1)S(1)}, u32[]{:S(2)}) copy-start(bf16[512,384]{1,0:T(8,128)(2,1)S(1)} %collective-permute-done.peer_ref) | copy-start | bytes 1179652

commit v2 on v1

v2 whole, which is shorter than its diff:
```python
import functools
import math

import jax
import jax.numpy as jnp
from jax import lax
from jax.experimental import pallas as pl
from jax.experimental.pallas import tpu as pltpu
from jax.sharding import PartitionSpec as P

LANES = 128
GROUPS = 8
VMEM_LIMIT = 20 * 2**20


def passed_along(value, axis, steps):
    count = lax.axis_size(axis)
    pairs = [(source, (source + steps) % count) for source in range(count)]
    return lax.ppermute(value, axis, pairs)


def swapped(value, axis, mask):
    count = lax.axis_size(axis)
    return lax.ppermute(value, axis, [(source, source ^ mask) for source in range(count)])


def divisor(value, limit):
    return max(d for d in range(1, min(value, limit) + 1) if value % d == 0)


def transfer_order(pairs):
    quarter = pairs // 4
    if quarter == 0:
        return list(range(1, pairs))
    far, near, corner = (range(quarter * k, quarter * (k + 1)) for k in (2, 1, 3))
    return [*far, *range(1, quarter), *near, *corner]


def arrival_order(pairs):
    quarter = pairs // 4
    if quarter == 0:
        return list(range(pairs))
    return [k for block in (0, 2, 1, 3) for k in range(quarter * block, quarter * (block + 1))]


def spectra_kernel(batch, segments, bins_ref, index_ref, gain_ref, traces_ref, keep_ref, send_ref, table, taper, held):
    step = pl.program_id(0)
    rows, length = table.shape
    nbins = rows // 2

    @pl.when(step == 0)
    def _():
        row = lax.broadcasted_iota(jnp.int32, (rows, length), 0)
        sample = lax.broadcasted_iota(jnp.int32, (rows, length), 1)
        bins = jnp.zeros((rows, length), jnp.int32)
        for k in range(nbins):
            core, pair = divmod(k, nbins // 2)
            bins = jnp.where(row // 2 == k, bins_ref[index_ref[0] ^ (2 * pair + core)], bins)
        phase = (bins * sample) & (length - 1)
        angle = 2.0 * math.pi / length * phase.astype(jnp.float32)
        wave = jnp.where(row % 2 == 0, jnp.cos(angle), -jnp.sin(angle))
        table[...] = wave.astype(jnp.bfloat16)
        place = lax.broadcasted_iota(jnp.int32, (8, length), 1).astype(jnp.float32)
        curve = 0.5 - 0.5 * jnp.cos(2.0 * math.pi / length * (place + 0.5))
        taper[...] = curve * math.sqrt(length)

    gain = gain_ref[...].astype(jnp.float32)
    for place in range(batch):
        record = traces_ref[place].astype(jnp.float32)
        squares = jnp.sum(record * record, axis=1, keepdims=True)
        inverse = lax.rsqrt(squares + 1e-06 * length)
        tapered = (record * inverse * taper[:1]).astype(jnp.bfloat16)
        spectra = lax.dot_general(
            table[...], tapered, (((1,), (1,)), ((), ())), preferred_element_type=jnp.float32
        )
        spectra = spectra * gain
        for tile in range(held.shape[0]):
            kept = spectra[:, tile * LANES : (tile + 1) * LANES]
            held[tile, pl.ds(step * batch + place, rows, stride=segments), :] = kept

    @pl.when(step == pl.num_programs(0) - 1)
    def _():
        half = rows * segments // 2
        for tile in range(held.shape[0]):
            lanes = slice(tile * LANES, (tile + 1) * LANES)
            keep_ref[:, lanes] = held[tile, :half].astype(jnp.bfloat16)
            send_ref[:, lanes] = held[tile, half:].astype(jnp.bfloat16)


def spectra_of(traces, channel_mask, bin_index, index):
    segments, width, length = traces.shape
    assert length & (length - 1) == 0
    rows = 2 * bin_index.shape[0]
    batch = divisor(segments, 2)
    half = jax.ShapeDtypeStruct((rows * segments // 2, width), jnp.bfloat16)
    return pl.pallas_call(
        functools.partial(spectra_kernel, batch, segments),
        grid_spec=pltpu.PrefetchScalarGridSpec(
            num_scalar_prefetch=2,
            grid=(segments // batch,),
            in_specs=[
                pl.BlockSpec((1, width), lambda i, *_: (0, 0)),
                pl.BlockSpec((batch, width, length), lambda i, *_: (i, 0, 0)),
            ],
            out_specs=[pl.BlockSpec(half.shape, lambda i, *_: (0, 0))] * 2,
            scratch_shapes=[
                pltpu.VMEM((rows, length), jnp.bfloat16),
                pltpu.VMEM((8, length), jnp.float32),
                pltpu.VMEM((width // LANES, rows * segments, LANES), jnp.float32),
            ],
        ),
        out_shape=[half, half],
        compiler_params=pltpu.CompilerParams(vmem_limit_bytes=VMEM_LIMIT),
        cost_estimate=pl.CostEstimate(
            flops=2 * rows * segments * width * length,
            bytes_accessed=2 * segments * width * length,
            transcendentals=0,
        ),
    )(bin_index, index, channel_mask[None, :], traces)


def gathered(refs, whole, across, segments):
    start = 0
    for ref in refs:
        whole[start : start + ref.shape[0]] = ref[...]
        start += ref.shape[0]
    wide = whole[...].astype(jnp.float32)
    across[...] = lax.rsqrt(jnp.sum(wide * wide, axis=0, keepdims=True) / segments + 1e-06)


def row_scale(values, segments):
    wide = values.astype(jnp.float32)
    power = jnp.sum(wide * wide, axis=1, keepdims=True) / segments
    return lax.rsqrt(power + 1e-06) * (1.0 / segments)


def own_kernel(local, segments, count, place_ref, *refs):
    own_refs, (out_ref, left_ref, whole, across) = refs[:count], refs[count:]
    step = pl.program_id(0)

    @pl.when(step == 0)
    def _():
        gathered(own_refs, whole, across, segments)

    rows = out_ref.shape[2]
    block = whole[:, pl.ds(pl.multiple_of(step * rows, rows), rows)]
    parts = block.reshape(block.shape[0] // (2 * local), 2, local, rows)
    turned = jnp.concatenate([parts[:, 1:], -parts[:, :1]], axis=1).reshape(block.shape)
    plain_left = block.T
    turned_left = turned.T
    here = pl.ds(pl.multiple_of(step * rows, rows), rows)
    left_ref[0, here] = plain_left
    left_ref[1, here] = turned_left
    scale = row_scale(plain_left, segments)
    for part, left in enumerate((plain_left, turned_left)):
        product = jnp.dot(left, whole[...], preferred_element_type=jnp.float32)
        out_ref[0, part] = (product * scale * across[...]).astype(jnp.bfloat16)


def own_blocks(own, local, place, group):
    depth = sum(piece.shape[0] for piece in own)
    width = own[0].shape[1]
    rows = divisor(width, 256)
    return pl.pallas_call(
        functools.partial(own_kernel, local, depth // 2, len(own)),
        grid_spec=pltpu.PrefetchScalarGridSpec(
            num_scalar_prefetch=1,
            grid=(width // rows,),
            in_specs=[pl.BlockSpec(memory_space=pltpu.VMEM)] * len(own),
            out_specs=[
                pl.BlockSpec((1, 2, rows, width), lambda i, at: (0, 0, i, at[0])),
                pl.BlockSpec(memory_space=pltpu.VMEM),
            ],
            scratch_shapes=[pltpu.VMEM((depth, width), jnp.bfloat16), pltpu.VMEM((1, width), jnp.float32)],
        ),
        out_shape=[
            jax.ShapeDtypeStruct((1, 2, width, group * width), jnp.bfloat16),
            jax.ShapeDtypeStruct((2, width, depth), jnp.bfloat16),
        ],
        compiler_params=pltpu.CompilerParams(vmem_limit_bytes=VMEM_LIMIT),
        cost_estimate=pl.CostEstimate(
            flops=4 * width * width * depth, bytes_accessed=4 * width * width, transcendentals=0
        ),
    )(place, *own)


def peer_kernel(segments, count, place_ref, left_ref, *refs):
    peer_refs, (_, out_ref, whole, across) = refs[:count], refs[count:]
    step = pl.program_id(0)

    @pl.when(step == 0)
    def _():
        gathered(peer_refs, whole, across, segments)

    rows = out_ref.shape[2]
    here = pl.ds(pl.multiple_of(step * rows, rows), rows)
    scale = row_scale(left_ref[0, here], segments)
    for part in range(2):
        product = jnp.dot(left_ref[part, here], whole[...], preferred_element_type=jnp.float32)
        out_ref[0, part] = (product * scale * across[...]).astype(jnp.bfloat16)


def peer_blocks(result, left, peer, place):
    _, width, depth = left.shape
    rows = divisor(width, 256)
    return pl.pallas_call(
        functools.partial(peer_kernel, depth // 2, len(peer)),
        grid_spec=pltpu.PrefetchScalarGridSpec(
            num_scalar_prefetch=1,
            grid=(width // rows,),
            in_specs=[
                *[pl.BlockSpec(memory_space=pltpu.VMEM)] * (1 + len(peer)),
                pl.BlockSpec(memory_space=pl.ANY),
            ],
            out_specs=pl.BlockSpec((1, 2, rows, width), lambda i, at: (0, 0, i, at[0])),
            scratch_shapes=[pltpu.VMEM((depth, width), jnp.bfloat16), pltpu.VMEM((1, width), jnp.float32)],
        ),
        out_shape=jax.ShapeDtypeStruct(result.shape, result.dtype),
        input_output_aliases={2 + len(peer): 0},
        compiler_params=pltpu.CompilerParams(vmem_limit_bytes=VMEM_LIMIT),
        cost_estimate=pl.CostEstimate(
            flops=4 * width * width * depth, bytes_accessed=4 * width * width, transcendentals=0
        ),
    )(place, left, *peer, result)


def shards(traces, channel_mask, bin_index):
    local, width, _ = traces.shape
    nbins = bin_index.shape[0]
    freq = lax.axis_size("freq")
    group = lax.axis_size("chan")
    own_index = lax.axis_index("chan")
    assert nbins == freq and freq & (freq - 1) == 0
    pairs = freq // 2
    depth = 2 * local

    index = lax.axis_index("freq")[None].astype(jnp.int32)
    keep, send = spectra_of(traces, channel_mask, bin_index, index)
    keep = keep.reshape(pairs, depth, width)
    got = swapped(send, "freq", 1).reshape(pairs, depth, width)
    arrived = {}
    for pair in [*transfer_order(pairs), 0]:
        both = jnp.concatenate([keep[pair], got[pair]], axis=0)
        arrived[pair] = swapped(both, "freq", 2 * pair) if pair else both
    order = arrival_order(pairs)
    each = max(1, pairs // GROUPS)
    own = []
    for start in range(0, pairs, each):
        members = [arrived[pair] for pair in order[start : start + each]]
        own.append(members[0] if each == 1 else jnp.concatenate(members, axis=0))
    moving = own
    moved = []
    for _ in range(1, group):
        for place in range(len(moving)):
            moving = [*moving[:place], passed_along(moving[place], "chan", 1), *moving[place + 1 :]]
        moved.append(moving)
    result, left = own_blocks(own, local, own_index[None].astype(jnp.int32), group)
    for step in range(1, group):
        owner = (own_index - step) % group
        result = peer_blocks(result, left, moved[step - 1], owner[None].astype(jnp.int32))
    return result


def solution(mesh):
    in_specs = (P("freq", "chan", None), P("chan"), P())
    out_specs = P("freq", None, "chan", None)
    return jax.shard_map(shards, mesh=mesh, in_specs=in_specs, out_specs=out_specs, check_vma=False)
```

time: 70.3 us -> 63 us (0.90)
  starting transfers between devices: 15.1 us -> 27.6 us
  Pallas kernels: 26.8 us -> 15.2 us
  waiting for transfers between devices: 22.5 us -> 14.9 us
  other arithmetic: 3.39 us -> 0.08 us
  local copies, waits for them, and re-layouts: 1.76 us -> 4.79 us
    all_to_all x2 -> x0, waiting for transfers between devices: 22.5 us -> none  [shards(): lax.all_to_all(blocks, 'freq', split_axis=0, concat_axis=0, tiled=True)]
    ppermute x0 -> x8, starting transfers between devices: none -> 17.5 us  [swapped(): lax.ppermute(value, axis, [(source, source ^ mask) for source in range(co...]
    all_to_all x2 -> x0, starting transfers between devices: 12.1 us -> none  [shards(): lax.all_to_all(blocks, 'freq', split_axis=0, concat_axis=0, tiled=True)]
    pallas_call x5 -> x3, Pallas kernels: 26.8 us -> 15.2 us  [the longest x1 6.52 us: spectra_of(): pl.pallas_call(functools.partial(spectra_kernel, batch, segments), grid_s...]
    ppermute x2 -> x8, waiting for transfers between devices: 0.01 us -> 8.72 us  [passed_along(): return lax.ppermute(value, axis, pairs)]
    ppermute x2 -> x8, starting transfers between devices: 3.05 us -> 10.2 us  [passed_along(): return lax.ppermute(value, axis, pairs)]
    ppermute x0 -> x8, waiting for transfers between devices: none -> 6.22 us  [swapped(): lax.ppermute(value, axis, [(source, source ^ mask) for source in range(co...]
    unnamed x8 -> x6, local copies, waits for them, and re-layouts: 1.61 us -> 4.72 us
  transfers between devices with their start and end apart: 4 -> 16, of which waited for: 2 -> 8; matrix products, arithmetic and copies ran while one was open for 0% -> 0% of each run, Pallas kernels for 23% -> 7%
where the time goes in v2:
time: 63 us; the launch traced here: 62.8 us
  starting transfers between devices  27.6 us (44%)
  Pallas kernels  15.2 us (24%)
  waiting for transfers between devices  14.9 us (24%)
  local copies, waits for them, and re-layouts  4.79 us (8%)
    ppermute x8, starting transfers between devices, swapped(): lax.ppermute(value, axis, [(source, source ^ mask) for source in range(co...  17.5 us
    ppermute x8, starting transfers between devices, passed_along(): return lax.ppermute(value, axis, pairs)  10.2 us
    ppermute x8, waiting for transfers between devices, passed_along(): return lax.ppermute(value, axis, pairs)  8.72 us
    pallas_call x1, Pallas kernels, spectra_of(): pl.pallas_call(functools.partial(spectra_kernel, batch, segments), grid_s...  6.52 us
    ppermute x8, waiting for transfers between devices, swapped(): lax.ppermute(value, axis, [(source, source ^ mask) for source in range(co...  6.22 us
    unnamed x6, local copies, waits for them, and re-layouts  4.72 us
    pallas_call x1, Pallas kernels, own_blocks(): pl.pallas_call(functools.partial(own_kernel, local, depth // 2, len(own))...  4.4 us
    pallas_call x1, Pallas kernels, peer_blocks(): pl.pallas_call(functools.partial(peer_kernel, depth // 2, len(peer)), gri...  4.32 us
  transfers between devices with their start and end apart: 16, of which 8 were waited for; matrix products, arithmetic and copies ran while one was open for 0% of the time, Pallas kernels for 7%

profile of v2, /device:TPU:0, one launch (start us, length us, event | category | flops | bytes accessed | tf_op | source)
XLA Modules:
  0.0 62.8 jit_solution(10866950834240745773)
XLA Ops:
  0.0 0.0 copy-start
  0.0 3.4 %copy-done = bf16[16,1024,256]{2,1,0:T(8,128)(2,1)S(1)} copy-done((bf16[16,1024,256]{2,1,0:T(8,128)(2,1)S(1)}, bf16[16,1024,256]{2,1,0:T(8,128)(2,1)}, u32[]{:S(2)}) %copy-start) | copy-done | bytes 8388632
  3.4 0.0 copy-start.1
  3.4 0.7 %copy-done.1 = s32[1024]{0:T(1024)S(1)} copy-done((s32[1024]{0:T(1024)S(1)}, s32[1024]{0:T(1024)}, u32[]{:S(2)}) %copy-start.1) | copy-done | bytes 4120
  4.1 0.0 copy-start.2
  4.1 0.7 %copy-done.2 = s32[16]{0:T(128)S(1)} copy-done((s32[16]{0:T(128)S(1)}, s32[16]{0:T(128)}, u32[]{:S(2)}) %copy-start.2) | copy-done | bytes 88
  4.7 6.5 %shard_map.37 = (bf16[256,1024]{1,0:T(8,128)(2,1)S(1)}, bf16[256,1024]{1,0:T(8,128)(2,1)S(1)}) custom-call(s32[16]{0:T(128)S(1)} %copy-done.2, s32[1]{0:T(128)} %bitcast.2.index_ref, s32[1,1024]{1,0:T(1,128)S(1)} %bitcast.4, bf16[16,1024,256]{2,1,0:T(8,128)(2,1)S(1)} %copy-done), custom_call_target="tpu_custom_call" | custom-call | flops 268435456 | bytes 8388608 | tf_op jit(solution)/shard_map/pallas_call | solution.py:96
  11.3 0.6 collective-permute-start
  11.8 1.5 %collective-permute-done = bf16[256,1024]{1,0:T(8,128)(2,1)S(1)} collective-permute-done((bf16[256,1024]{1,0:T(8,128)(2,1)S(1)}, bf16[256,1024]{1,0:T(8,128)(2,1)S(1)}, u32[]{:S(2)}, u32[]{:S(2)}) %collective-permute-start) | collective-permute-done | bytes 524320 | tf_op jit(solution)/shard_map/ppermute | solution.py:24
  13.4 2.9 %collective-permute-start.1 = (bf16[64,1024]{1,0:T(8,128)(2,1)S(1)}, bf16[64,1024]{1,0:T(8,128)(2,1)S(1)}, u32[]{:S(2)}, u32[]{:S(2)}) collective-permute-start(bf16[64,1024]{1,0:T(8,128)(2,1)S(1)} %pad_maximum_fusion.1), channel_id=1, source_target_pairs={{0,4},{2,6},{4,0},{6,2},{8,12},{10,14},{12,8},{14,10},{16,20},{18,... | collective-permute-start | bytes 393224 | tf_op jit(solution)/shard_map/ppermute | solution.py:24
  16.4 2.7 %collective-permute-start.2 = (bf16[64,1024]{1,0:T(8,128)(2,1)S(1)}, bf16[64,1024]{1,0:T(8,128)(2,1)S(1)}, u32[]{:S(2)}, u32[]{:S(2)}) collective-permute-start(bf16[64,1024]{1,0:T(8,128)(2,1)S(1)} %pad_maximum_fusion.2), channel_id=1, source_target_pairs={{0,16},{2,18},{4,20},{6,22},{8,24},{10,26},{12,28},{14,30},{16,0},... | collective-permute-start | bytes 393224 | tf_op jit(solution)/shard_map/ppermute | solution.py:24
  19.0 0.1 collective-permute-start.3
  19.1 1.9 %collective-permute-start.4 = (bf16[64,1024]{1,0:T(8,128)(2,1)S(1)}, bf16[64,1024]{1,0:T(8,128)(2,1)S(1)}, u32[]{:S(2)}, u32[]{:S(2)}) collective-permute-start(bf16[64,1024]{1,0:T(8,128)(2,1)S(1)} %pad_maximum_fusion.4), channel_id=1, source_target_pairs={{0,8},{2,10},{4,12},{6,14},{8,0},{10,2},{12,4},{14,6},{16,24},{18,... | collective-permute-start | bytes 393224 | tf_op jit(solution)/shard_map/ppermute | solution.py:24
  21.0 1.5 %collective-permute-start.5 = (bf16[64,1024]{1,0:T(8,128)(2,1)S(1)}, bf16[64,1024]{1,0:T(8,128)(2,1)S(1)}, u32[]{:S(2)}, u32[]{:S(2)}) collective-permute-start(bf16[64,1024]{1,0:T(8,128)(2,1)S(1)} %pad_maximum_fusion.5), channel_id=1, source_target_pairs={{0,12},{2,14},{4,8},{6,10},{8,4},{10,6},{12,0},{14,2},{16,28},{18,... | collective-permute-start | bytes 393224 | tf_op jit(solution)/shard_map/ppermute | solution.py:24
  22.6 0.0 collective-permute-done.1.refs_1_
  22.6 3.7 %collective-permute-start.6 = (bf16[64,1024]{1,0:T(8,128)(2,1)S(1)}, bf16[64,1024]{1,0:T(8,128)(2,1)S(1)}, u32[]{:S(2)}, u32[]{:S(2)}) collective-permute-start(bf16[64,1024]{1,0:T(8,128)(2,1)S(1)} %pad_maximum_fusion.6), channel_id=1, source_target_pairs={{0,24},{2,26},{4,28},{6,30},{8,16},{10,18},{12,20},{14,22},{16,8},... | collective-permute-start | bytes 393224 | tf_op jit(solution)/shard_map/ppermute | solution.py:24
  26.2 3.2 %collective-permute-done.2.refs_2_ = bf16[64,1024]{1,0:T(8,128)(2,1)S(1)} collective-permute-done((bf16[64,1024]{1,0:T(8,128)(2,1)S(1)}, bf16[64,1024]{1,0:T(8,128)(2,1)S(1)}, u32[]{:S(2)}, u32[]{:S(2)}) %collective-permute-start.2) | collective-permute-done | bytes 131104 | tf_op jit(solution)/shard_map/ppermute | solution.py:24
  29.4 1.5 %collective-permute-start.8 = (bf16[64,1024]{1,0:T(8,128)(2,1)S(1)}, bf16[64,1024]{1,0:T(8,128)(2,1)S(1)}, u32[]{:S(2)}, u32[]{:S(2)}) collective-permute-start(bf16[64,1024]{1,0:T(8,128)(2,1)S(1)} %pad_maximum_fusion.refs_0_), channel_id=1, source_target_pairs={{0,1},{1,0},{2,3},{3,2},{4,5},{5,4},{6,7},{7,6},{8,9},{9,8},{10,11... | collective-permute-start | bytes 393224 | tf_op jit(solution)/shard_map/ppermute | solution.py:19
  30.9 1.5 %collective-permute-done.3.refs_3_ = bf16[64,1024]{1,0:T(8,128)(2,1)S(1)} collective-permute-done((bf16[64,1024]{1,0:T(8,128)(2,1)S(1)}, bf16[64,1024]{1,0:T(8,128)(2,1)S(1)}, u32[]{:S(2)}, u32[]{:S(2)}) %collective-permute-start.3) | collective-permute-done | bytes 131104 | tf_op jit(solution)/shard_map/ppermute | solution.py:24
  32.4 4.2 %collective-permute-start.7 = (bf16[64,1024]{1,0:T(8,128)(2,1)S(1)}, bf16[64,1024]{1,0:T(8,128)(2,1)S(1)}, u32[]{:S(2)}, u32[]{:S(2)}) collective-permute-start(bf16[64,1024]{1,0:T(8,128)(2,1)S(1)} %pad_maximum_fusion.7), channel_id=1, source_target_pairs={{0,28},{2,30},{4,24},{6,26},{8,20},{10,22},{12,16},{14,18},{16,12}... | collective-permute-start | bytes 393224 | tf_op jit(solution)/shard_map/ppermute | solution.py:24
  36.7 0.0 collective-permute-done.4.refs_4_
  36.7 1.5 %collective-permute-start.9 = (bf16[64,1024]{1,0:T(8,128)(2,1)S(1)}, bf16[64,1024]{1,0:T(8,128)(2,1)S(1)}, u32[]{:S(2)}, u32[]{:S(2)}) collective-permute-start(bf16[64,1024]{1,0:T(8,128)(2,1)S(1)} %collective-permute-done.1.refs_1_), channel_id=1, source_target_pairs={{0,1},{1,0},{2,3},{3,2},{4,5},{5,4},{6,7},{7,6},{8,9},{9,8},{10,11... | collective-permute-start | bytes 393224 | tf_op jit(solution)/shard_map/ppermute | solution.py:19
  38.2 0.0 collective-permute-done.5.refs_5_
  38.2 0.5 collective-permute-start.10
  38.7 0.0 collective-permute-done.6.refs_6_
  38.7 1.5 %collective-permute-start.11 = (bf16[64,1024]{1,0:T(8,128)(2,1)S(1)}, bf16[64,1024]{1,0:T(8,128)(2,1)S(1)}, u32[]{:S(2)}, u32[]{:S(2)}) collective-permute-start(bf16[64,1024]{1,0:T(8,128)(2,1)S(1)} %collective-permute-done.3.refs_3_), channel_id=1, source_target_pairs={{0,1},{1,0},{2,3},{3,2},{4,5},{5,4},{6,7},{7,6},{8,9},{9,8},{10,11... | collective-permute-start | bytes 393224 | tf_op jit(solution)/shard_map/ppermute | solution.py:19
  40.2 0.0 collective-permute-done.8.refs_0_
  40.2 0.5 collective-permute-start.12
  40.7 0.0 collective-permute-done.7.refs_7_
  40.7 1.6 %collective-permute-start.13 = (bf16[64,1024]{1,0:T(8,128)(2,1)S(1)}, bf16[64,1024]{1,0:T(8,128)(2,1)S(1)}, u32[]{:S(2)}, u32[]{:S(2)}) collective-permute-start(bf16[64,1024]{1,0:T(8,128)(2,1)S(1)} %collective-permute-done.5.refs_5_), channel_id=1, source_target_pairs={{0,1},{1,0},{2,3},{3,2},{4,5},{5,4},{6,7},{7,6},{8,9},{9,8},{10,11... | collective-permute-start | bytes 393224 | tf_op jit(solution)/shard_map/ppermute | solution.py:19
  42.4 0.7 %collective-permute-done.9.refs_1_ = bf16[64,1024]{1,0:T(8,128)(2,1)S(1)} collective-permute-done((bf16[64,1024]{1,0:T(8,128)(2,1)S(1)}, bf16[64,1024]{1,0:T(8,128)(2,1)S(1)}, u32[]{:S(2)}, u32[]{:S(2)}) %collective-permute-start.9) | collective-permute-done | bytes 131104 | tf_op jit(solution)/shard_map/ppermute | solution.py:19
  43.0 1.5 %collective-permute-start.14 = (bf16[64,1024]{1,0:T(8,128)(2,1)S(1)}, bf16[64,1024]{1,0:T(8,128)(2,1)S(1)}, u32[]{:S(2)}, u32[]{:S(2)}) collective-permute-start(bf16[64,1024]{1,0:T(8,128)(2,1)S(1)} %collective-permute-done.6.refs_6_), channel_id=1, source_target_pairs={{0,1},{1,0},{2,3},{3,2},{4,5},{5,4},{6,7},{7,6},{8,9},{9,8},{10,11... | collective-permute-start | bytes 393224 | tf_op jit(solution)/shard_map/ppermute | solution.py:19
  44.5 1.3 %collective-permute-done.10.refs_2_ = bf16[64,1024]{1,0:T(8,128)(2,1)S(1)} collective-permute-done((bf16[64,1024]{1,0:T(8,128)(2,1)S(1)}, bf16[64,1024]{1,0:T(8,128)(2,1)S(1)}, u32[]{:S(2)}, u32[]{:S(2)}) %collective-permute-start.10) | collective-permute-done | bytes 131104 | tf_op jit(solution)/shard_map/ppermute | solution.py:19
  45.8 1.5 %collective-permute-start.15 = (bf16[64,1024]{1,0:T(8,128)(2,1)S(1)}, bf16[64,1024]{1,0:T(8,128)(2,1)S(1)}, u32[]{:S(2)}, u32[]{:S(2)}) collective-permute-start(bf16[64,1024]{1,0:T(8,128)(2,1)S(1)} %collective-permute-done.7.refs_7_), channel_id=1, source_target_pairs={{0,1},{1,0},{2,3},{3,2},{4,5},{5,4},{6,7},{7,6},{8,9},{9,8},{10,11... | collective-permute-start | bytes 393224 | tf_op jit(solution)/shard_map/ppermute | solution.py:19
  47.3 4.4 %shard_map.38 = (bf16[1,2,1024,2048]{3,2,1,0:T(8,128)(2,1)}, bf16[2,1024,512]{2,1,0:T(8,128)(2,1)S(1)}) custom-call(s32[1]{0:T(128)} %bitcast.1.place_ref, bf16[64,1024]{1,0:T(8,128)(2,1)S(1)} %pad_maximum_fusion.refs_0_, bf16[64,1024]{1,0:T(8,128)(2,1)S(1)} %collective-permute-done.1.refs_1_, bf16[64,1024]{1,0:T(8,128)(2,1)S(1)} %collective-permute-done.2.refs_2_, ...), custom_call_target="tpu_custom_call" | custom-call | flops 2147483648 | bytes 4194304 | tf_op jit(solution)/shard_map/pallas_call | solution.py:164
  51.7 0.0 collective-permute-done.11.refs_3_
  51.7 0.0 collective-permute-done.12.refs_4_
  51.7 2.5 %collective-permute-done.13.refs_5_ = bf16[64,1024]{1,0:T(8,128)(2,1)S(1)} collective-permute-done((bf16[64,1024]{1,0:T(8,128)(2,1)S(1)}, bf16[64,1024]{1,0:T(8,128)(2,1)S(1)}, u32[]{:S(2)}, u32[]{:S(2)}) %collective-permute-start.13) | collective-permute-done | bytes 131104 | tf_op jit(solution)/shard_map/ppermute | solution.py:19
  54.3 2.8 %collective-permute-done.14.refs_6_ = bf16[64,1024]{1,0:T(8,128)(2,1)S(1)} collective-permute-done((bf16[64,1024]{1,0:T(8,128)(2,1)S(1)}, bf16[64,1024]{1,0:T(8,128)(2,1)S(1)}, u32[]{:S(2)}, u32[]{:S(2)}) %collective-permute-start.14) | collective-permute-done | bytes 131104 | tf_op jit(solution)/shard_map/ppermute | solution.py:19
  57.0 1.4 %collective-permute-done.15.refs_7_ = bf16[64,1024]{1,0:T(8,128)(2,1)S(1)} collective-permute-done((bf16[64,1024]{1,0:T(8,128)(2,1)S(1)}, bf16[64,1024]{1,0:T(8,128)(2,1)S(1)}, u32[]{:S(2)}, u32[]{:S(2)}) %collective-permute-start.15) | collective-permute-done | bytes 131104 | tf_op jit(solution)/shard_map/ppermute | solution.py:19
  58.4 4.3 %shard_map.39 = bf16[1,2,1024,2048]{3,2,1,0:T(8,128)(2,1)} custom-call(s32[1]{0:T(128)} %bitcast.place_ref, bf16[2,1024,512]{2,1,0:T(8,128)(2,1)S(1)} %get-tuple-element.11.left_ref, bf16[64,1024]{1,0:T(8,128)(2,1)S(1)} %collective-permute-done.8.refs_0_, bf16[64,1024]{1,0:T(8,128)(2,1)S(1)} %collective-permute-done.9.refs_1_, ...), custom_call_target="tpu_custom_call", output_to_operand_aliasing={{}: (10, {})} | custom-call | flops 2147483648 | bytes 4194304 | tf_op jit(solution)/shard_map/pallas_call | solution.py:206
  (10 shorter events, 0.2 us)
Async XLA Ops:
  0.0 3.4 %copy-start = (bf16[16,1024,256]{2,1,0:T(8,128)(2,1)S(1)}, bf16[16,1024,256]{2,1,0:T(8,128)(2,1)}, u32[]{:S(2)}) copy-start(bf16[16,1024,256]{2,1,0:T(8,128)(2,1)} %traces_ref.1) | copy-start | bytes 25165828
  3.4 0.7 %copy-start.1 = (s32[1024]{0:T(1024)S(1)}, s32[1024]{0:T(1024)}, u32[]{:S(2)}) copy-start(s32[1024]{0:T(1024)} %param.4) | copy-start | bytes 12292
  4.1 0.7 %copy-start.2 = (s32[16]{0:T(128)S(1)}, s32[16]{0:T(128)}, u32[]{:S(2)}) copy-start(s32[16]{0:T(128)} %bins_ref.1) | copy-start | bytes 196
  11.3 2.1 %collective-permute-start = (bf16[256,1024]{1,0:T(8,128)(2,1)S(1)}, bf16[256,1024]{1,0:T(8,128)(2,1)S(1)}, u32[]{:S(2)}, u32[]{:S(2)}) collective-permute-start(bf16[256,1024]{1,0:T(8,128)(2,1)S(1)} %get-tuple-element.10), channel_id=1, source_target_pairs={{0,2},{2,0},{4,6},{6,4},{8,10},{10,8},{12,14},{14,12},{16,18},{18,... | collective-permute-start | bytes 1572872 | tf_op jit(solution)/shard_map/ppermute | solution.py:24
  13.4 9.2 %collective-permute-start.1 = (bf16[64,1024]{1,0:T(8,128)(2,1)S(1)}, bf16[64,1024]{1,0:T(8,128)(2,1)S(1)}, u32[]{:S(2)}, u32[]{:S(2)}) collective-permute-start(bf16[64,1024]{1,0:T(8,128)(2,1)S(1)} %pad_maximum_fusion.1), channel_id=1, source_target_pairs={{0,4},{2,6},{4,0},{6,2},{8,12},{10,14},{12,8},{14,10},{16,20},{18,... | collective-permute-start | bytes 393224 | tf_op jit(solution)/shard_map/ppermute | solution.py:24
  16.4 13.0 %collective-permute-start.2 = (bf16[64,1024]{1,0:T(8,128)(2,1)S(1)}, bf16[64,1024]{1,0:T(8,128)(2,1)S(1)}, u32[]{:S(2)}, u32[]{:S(2)}) collective-permute-start(bf16[64,1024]{1,0:T(8,128)(2,1)S(1)} %pad_maximum_fusion.2), channel_id=1, source_target_pairs={{0,16},{2,18},{4,20},{6,22},{8,24},{10,26},{12,28},{14,30},{16,0},... | collective-permute-start | bytes 393224 | tf_op jit(solution)/shard_map/ppermute | solution.py:24
  19.0 13.4 %collective-permute-start.3 = (bf16[64,1024]{1,0:T(8,128)(2,1)S(1)}, bf16[64,1024]{1,0:T(8,128)(2,1)S(1)}, u32[]{:S(2)}, u32[]{:S(2)}) collective-permute-start(bf16[64,1024]{1,0:T(8,128)(2,1)S(1)} %pad_maximum_fusion.3), channel_id=1, source_target_pairs={{0,20},{2,22},{4,16},{6,18},{8,28},{10,30},{12,24},{14,26},{16,4},... | collective-permute-start | bytes 393224 | tf_op jit(solution)/shard_map/ppermute | solution.py:24
  19.1 17.5 %collective-permute-start.4 = (bf16[64,1024]{1,0:T(8,128)(2,1)S(1)}, bf16[64,1024]{1,0:T(8,128)(2,1)S(1)}, u32[]{:S(2)}, u32[]{:S(2)}) collective-permute-start(bf16[64,1024]{1,0:T(8,128)(2,1)S(1)} %pad_maximum_fusion.4), channel_id=1, source_target_pairs={{0,8},{2,10},{4,12},{6,14},{8,0},{10,2},{12,4},{14,6},{16,24},{18,... | collective-permute-start | bytes 393224 | tf_op jit(solution)/shard_map/ppermute | solution.py:24
  21.0 17.1 %collective-permute-start.5 = (bf16[64,1024]{1,0:T(8,128)(2,1)S(1)}, bf16[64,1024]{1,0:T(8,128)(2,1)S(1)}, u32[]{:S(2)}, u32[]{:S(2)}) collective-permute-start(bf16[64,1024]{1,0:T(8,128)(2,1)S(1)} %pad_maximum_fusion.5), channel_id=1, source_target_pairs={{0,12},{2,14},{4,8},{6,10},{8,4},{10,6},{12,0},{14,2},{16,28},{18,... | collective-permute-start | bytes 393224 | tf_op jit(solution)/shard_map/ppermute | solution.py:24
  22.6 16.1 %collective-permute-start.6 = (bf16[64,1024]{1,0:T(8,128)(2,1)S(1)}, bf16[64,1024]{1,0:T(8,128)(2,1)S(1)}, u32[]{:S(2)}, u32[]{:S(2)}) collective-permute-start(bf16[64,1024]{1,0:T(8,128)(2,1)S(1)} %pad_maximum_fusion.6), channel_id=1, source_target_pairs={{0,24},{2,26},{4,28},{6,30},{8,16},{10,18},{12,20},{14,22},{16,8},... | collective-permute-start | bytes 393224 | tf_op jit(solution)/shard_map/ppermute | solution.py:24
  29.4 10.8 %collective-permute-start.8 = (bf16[64,1024]{1,0:T(8,128)(2,1)S(1)}, bf16[64,1024]{1,0:T(8,128)(2,1)S(1)}, u32[]{:S(2)}, u32[]{:S(2)}) collective-permute-start(bf16[64,1024]{1,0:T(8,128)(2,1)S(1)} %pad_maximum_fusion.refs_0_), channel_id=1, source_target_pairs={{0,1},{1,0},{2,3},{3,2},{4,5},{5,4},{6,7},{7,6},{8,9},{9,8},{10,11... | collective-permute-start | bytes 393224 | tf_op jit(solution)/shard_map/ppermute | solution.py:19
  32.4 8.3 %collective-permute-start.7 = (bf16[64,1024]{1,0:T(8,128)(2,1)S(1)}, bf16[64,1024]{1,0:T(8,128)(2,1)S(1)}, u32[]{:S(2)}, u32[]{:S(2)}) collective-permute-start(bf16[64,1024]{1,0:T(8,128)(2,1)S(1)} %pad_maximum_fusion.7), channel_id=1, source_target_pairs={{0,28},{2,30},{4,24},{6,26},{8,20},{10,22},{12,16},{14,18},{16,12}... | collective-permute-start | bytes 393224 | tf_op jit(solution)/shard_map/ppermute | solution.py:24
  36.7 6.4 %collective-permute-start.9 = (bf16[64,1024]{1,0:T(8,128)(2,1)S(1)}, bf16[64,1024]{1,0:T(8,128)(2,1)S(1)}, u32[]{:S(2)}, u32[]{:S(2)}) collective-permute-start(bf16[64,1024]{1,0:T(8,128)(2,1)S(1)} %collective-permute-done.1.refs_1_), channel_id=1, source_target_pairs={{0,1},{1,0},{2,3},{3,2},{4,5},{5,4},{6,7},{7,6},{8,9},{9,8},{10,11... | collective-permute-start | bytes 393224 | tf_op jit(solution)/shard_map/ppermute | solution.py:19
  38.2 7.7 %collective-permute-start.10 = (bf16[64,1024]{1,0:T(8,128)(2,1)S(1)}, bf16[64,1024]{1,0:T(8,128)(2,1)S(1)}, u32[]{:S(2)}, u32[]{:S(2)}) collective-permute-start(bf16[64,1024]{1,0:T(8,128)(2,1)S(1)} %collective-permute-done.2.refs_2_), channel_id=1, source_target_pairs={{0,1},{1,0},{2,3},{3,2},{4,5},{5,4},{6,7},{7,6},{8,9},{9,8},{10,11... | collective-permute-start | bytes 393224 | tf_op jit(solution)/shard_map/ppermute | solution.py:19
  38.7 13.0 %collective-permute-start.11 = (bf16[64,1024]{1,0:T(8,128)(2,1)S(1)}, bf16[64,1024]{1,0:T(8,128)(2,1)S(1)}, u32[]{:S(2)}, u32[]{:S(2)}) collective-permute-start(bf16[64,1024]{1,0:T(8,128)(2,1)S(1)} %collective-permute-done.3.refs_3_), channel_id=1, source_target_pairs={{0,1},{1,0},{2,3},{3,2},{4,5},{5,4},{6,7},{7,6},{8,9},{9,8},{10,11... | collective-permute-start | bytes 393224 | tf_op jit(solution)/shard_map/ppermute | solution.py:19
  40.2 11.5 %collective-permute-start.12 = (bf16[64,1024]{1,0:T(8,128)(2,1)S(1)}, bf16[64,1024]{1,0:T(8,128)(2,1)S(1)}, u32[]{:S(2)}, u32[]{:S(2)}) collective-permute-start(bf16[64,1024]{1,0:T(8,128)(2,1)S(1)} %collective-permute-done.4.refs_4_), channel_id=1, source_target_pairs={{0,1},{1,0},{2,3},{3,2},{4,5},{5,4},{6,7},{7,6},{8,9},{9,8},{10,11... | collective-permute-start | bytes 393224 | tf_op jit(solution)/shard_map/ppermute | solution.py:19
  40.7 13.5 %collective-permute-start.13 = (bf16[64,1024]{1,0:T(8,128)(2,1)S(1)}, bf16[64,1024]{1,0:T(8,128)(2,1)S(1)}, u32[]{:S(2)}, u32[]{:S(2)}) collective-permute-start(bf16[64,1024]{1,0:T(8,128)(2,1)S(1)} %collective-permute-done.5.refs_5_), channel_id=1, source_target_pairs={{0,1},{1,0},{2,3},{3,2},{4,5},{5,4},{6,7},{7,6},{8,9},{9,8},{10,11... | collective-permute-start | bytes 393224 | tf_op jit(solution)/shard_map/ppermute | solution.py:19
  43.0 14.0 %collective-permute-start.14 = (bf16[64,1024]{1,0:T(8,128)(2,1)S(1)}, bf16[64,1024]{1,0:T(8,128)(2,1)S(1)}, u32[]{:S(2)}, u32[]{:S(2)}) collective-permute-start(bf16[64,1024]{1,0:T(8,128)(2,1)S(1)} %collective-permute-done.6.refs_6_), channel_id=1, source_target_pairs={{0,1},{1,0},{2,3},{3,2},{4,5},{5,4},{6,7},{7,6},{8,9},{9,8},{10,11... | collective-permute-start | bytes 393224 | tf_op jit(solution)/shard_map/ppermute | solution.py:19
  45.8 12.6 %collective-permute-start.15 = (bf16[64,1024]{1,0:T(8,128)(2,1)S(1)}, bf16[64,1024]{1,0:T(8,128)(2,1)S(1)}, u32[]{:S(2)}, u32[]{:S(2)}) collective-permute-start(bf16[64,1024]{1,0:T(8,128)(2,1)S(1)} %collective-permute-done.7.refs_7_), channel_id=1, source_target_pairs={{0,1},{1,0},{2,3},{3,2},{4,5},{5,4},{6,7},{7,6},{8,9},{9,8},{10,11... | collective-permute-start | bytes 393224 | tf_op jit(solution)/shard_map/ppermute | solution.py:19
